TPU v7x, 256 devices: a whole 4x4x8 slice. The times are simulated.
256 devices in a mesh: vec: 16 (over z, y_lo), grid: 16 (over x, y_hi, core).
Axes of the slice: x: 4, y: 4 (y_hi: 2, y_lo: 2; y = y_hi * 2 + y_lo), z: 8, core: 2. Of those that a mesh axis runs over, the one named last changes fastest.
Arguments:
- fitting_vectors: float32 [256, 32, 1024], P('vec', 'grid'), may hold values from -6 to 6
Outputs:
- coulomb_blocks: float32 [256, 9, 16], P(('vec', 'grid'))
All inputs are finite; a program needn't handle non-finite values.
Results may differ from a plain program's by a relative error of at most 0.00005.
Values sent between devices are 32-bit elements; how exact they have to be, the bound alone decides.
A program may use at most 64 MiB of HBM per device.

v0:
```python
import functools
import math

import jax
import jax.numpy as jnp
import numpy as np
from jax import lax
from jax.experimental import pallas as pl
from jax.experimental.pallas import tpu as pltpu
from jax.sharding import PartitionSpec as P

N = 32
PAD = 2 * N
F32 = jnp.float32
BF16 = jnp.bfloat16
MESH = pl.DeviceIdType.MESH
REACH = 4


def tables():
    pos = np.arange(N) - (N - 1) / 2.0
    freqs = np.concatenate([np.arange(N), np.arange(1, N + 1)])
    phase = 2.0 * np.pi * freqs[:, None] * pos[None, :] / PAD
    trig = np.where(np.arange(PAD)[:, None] < N, np.cos(phase), np.sin(phase))
    weight = np.where((freqs == 0) | (freqs == N), 1.0, 2.0)
    f = freqs.astype(np.float64)
    total = f[:, None, None] ** 2 + f[None, :, None] ** 2 + f[None, None, :] ** 2
    g2 = total * (2.0 * np.pi / PAD) ** 2
    safe = np.where(total > 0, g2, 1.0)
    kernel = 8.0 * np.pi * np.sin(np.sqrt(safe) * (N / 2)) ** 2 / safe
    kernel = np.where(total > 0, kernel, 2.0 * np.pi * N * N)
    kernel = kernel * weight[:, None, None] * weight[None, :, None] * weight[None, None, :]
    kernel = kernel / float(PAD) ** 3 / float(N) ** 3
    return trig, kernel


def split_np(a):
    hi = a.astype(np.float32).astype(BF16)
    lo = (a - hi.astype(np.float64)).astype(np.float32).astype(BF16)
    return hi, lo


def constants():
    trig, kernel = tables()
    row = np.arange(N)
    y_of_row = 4 * (row % 8) + row // 8
    ty = trig[:, y_of_row]
    hi, lo = split_np(ty)
    ly = np.concatenate([hi, hi, lo], axis=1)
    hi, lo = split_np(ty.T)
    lyi = np.concatenate([hi, hi, lo], axis=1)
    hi, lo = split_np(np.kron(np.eye(8), trig.T))
    bz = np.stack([hi, lo])
    hi, lo = split_np(np.kron(np.eye(4), trig))
    bzi = np.concatenate([hi, lo], axis=1)
    kt = kernel.reshape(8, 8, PAD, PAD).transpose(0, 2, 1, 3).reshape(8 * PAD, 8 * PAD)
    return ly, lyi, bz, bzi, kt.astype(np.float32), trig


def split(x):
    hi = x.astype(BF16)
    lo = (x - hi.astype(F32)).astype(BF16)
    return hi, lo


def dot(a, b):
    return jnp.dot(a, b, preferred_element_type=F32)


def dot_nt(a, b):
    return lax.dot_general(a, b, (((1,), (1,)), ((), ())), preferred_element_type=F32)


def combine(matrix, values):
    out = []
    for weights in matrix:
        acc = None
        for w, v in zip(weights, values):
            term = v * np.float32(w)
            acc = term if acc is None else acc + term
        out.append(acc)
    return out


def swap_chunks(tiles, odd1, odd2):
    t0, t1, t2, t3 = tiles

    def pair(a, b, mask, up, down):
        return (
            jnp.where(mask, pltpu.roll(b, up, 1), a),
            jnp.where(mask, b, pltpu.roll(a, down, 1)),
        )

    a0, a1 = pair(t0, t1, odd1, 32, 96)
    a2, a3 = pair(t2, t3, odd1, 32, 96)
    b0, b2 = pair(a0, a2, odd2, 64, 64)
    b1, b3 = pair(a1, a3, odd2, 64, 64)
    return b0, b1, b2, b3


def body_kernel(
    trig,
    v_in, ly_in, lyi_in, bz_in, bzi_in, kt_in,
    out_ref,
    u, pbuf, pl_in, vl, ly, lyi, bz, bzi, kt,
    m1, m2h, m2l, m3h, m3l, m4, m5, vh, vlo, sb, rl,
    c_sem, a1_send, a1_recv, v_send, v_recv, v_loc, a2_send, a2_recv, a2_loc, r_send, r_recv, r_loc,
):
    g = lax.axis_index("vec")
    r = lax.axis_index("grid")
    half = lax.rem(g, 2)
    sib = g + 1 - 2 * half
    down = lax.rem(g + 14, 16)
    down_sib = lax.rem(sib + 14, 16)
    up = lax.rem(g + 2, 16)
    up_sib = lax.rem(sib + 2, 16)
    base = g - half
    me = half * 16 + r

    consts = [
        pltpu.make_async_copy(a, b, c_sem.at[i])
        for i, (a, b) in enumerate([(ly_in, ly), (lyi_in, lyi), (bz_in, bz), (bzi_in, bzi), (kt_in, kt)])
    ]
    for c in consts:
        c.start()
    own = pltpu.make_async_copy(
        v_in.at[:, pl.ds(8 * half, 8), :], vl.at[pl.ds(16 * half, 16)], v_loc
    )
    own.start()

    barrier = pltpu.get_barrier_semaphore()

    def greet(i, _):
        p = lax.rem(me + i, 32)
        pl.semaphore_signal(
            barrier, inc=1, device_id=(base + p // 16, lax.rem(p, 16)), device_id_type=MESH
        )
        return 0

    lax.fori_loop(1, 32, greet, 0)
    for other in (down, down_sib, up, up_sib):
        pl.semaphore_signal(barrier, inc=1, device_id=(other, r), device_id_type=MESH)
    pl.semaphore_wait(barrier, 35)

    def send_slab(m, _):
        pltpu.make_async_remote_copy(
            v_in.at[m], u.at[pl.ds(16 * r, 16)], a1_send, a1_recv,
            device_id=(sib, m), device_id_type=MESH,
        ).start()
        return 0

    lax.fori_loop(0, 16, send_slab, 0)

    def move(src, d, part, sem, target):
        return pltpu.make_async_remote_copy(
            src, vl.at[pl.ds(32 * d + 16 * part, 16)], v_send.at[sem], v_recv.at[sem],
            device_id=(target, r), device_id_type=MESH,
        )

    mine = v_in.at[:, pl.ds(8 * half, 8), :]
    other = v_in.at[:, pl.ds(8 * (1 - half), 8), :]
    first = [
        move(mine, 1, half, 1, down),
        move(other, 1, half, 2, down_sib),
        move(other, 0, half, 0, sib),
    ]
    for c in first:
        c.start()

    def wait_part(d, part, sem):
        ref = vl.at[pl.ds(32 * d + 16 * part, 16)]
        pltpu.make_async_copy(ref, ref, v_recv.at[sem]).wait()

    def relay(d):
        for k in range(2):
            part = half if k == 0 else 1 - half
            wait_part(d, part, 2 * d - 1 + k)
            if d < REACH:
                ref = vl.at[pl.ds(32 * d + 16 * part, 16)]
                move(ref, d + 1, part, 2 * d + 1 + k, down).start()

    relay(1)
    for c in consts:
        c.wait()
    pltpu.make_async_copy(u, u, a1_recv).wait()

    lane = lax.broadcasted_iota(jnp.int32, (8, 128), 1) // 32
    odd1 = lane % 2 == 1
    odd2 = lane >= 2

    def plane(x):
        return u[pl.ds(16 * (x // 2) + x % 2, 8, stride=2), :]

    low = [plane(15 - n) for n in range(16)]
    high = [plane(16 + n) for n in range(16)]
    for part in range(2):
        if part == 0:
            vals = [a + b for a, b in zip(high, low)]
        else:
            vals = [a - b for a, b in zip(high, low)]
        for a in range(8):
            q = 32 * part + 4 * a
            tiles = combine(trig[q:q + 4, 16:32], vals)
            tile = jnp.concatenate(swap_chunks(tiles, odd1, odd2), axis=0)
            hi, lo = split(tile)
            cols = pl.ds((8 * part + a) * 128, 128)
            m1[0:32, cols] = hi
            m1[32:64, cols] = lo
            m1[64:96, cols] = hi

    for n in range(8):
        hi, lo = split(dot(ly[...], m1[:, 256 * n:256 * n + 256]))
        m2h[64 * n:64 * n + 64, :] = hi
        m2l[64 * n:64 * n + 64, :] = lo

    for n in range(4):
        rows = slice(128 * n, 128 * n + 128)
        t = dot(m2h[rows, :], bz[0]) + dot(m2l[rows, :], bz[0]) + dot(m2h[rows, :], bz[1])
        hi, lo = split(t * kt[rows, :])
        m3h[rows, :] = hi
        m3l[rows, :] = lo

    relay(2)

    for n in range(8):
        rows = slice(64 * n, 64 * n + 64)
        for h in range(2):
            cols = slice(256 * h, 256 * h + 256)
            w = dot(m3h[rows, cols], bzi[...])
            t = w[:, 0:128] + w[:, 128:256] + dot(m3l[rows, cols], bzi[:, 0:128])
            hi, lo = split(t)
            out = pl.ds((2 * n + h) * 128, 128)
            m4[0:64, out] = hi
            m4[64:128, out] = lo
            m4[128:192, out] = hi

    for n in range(8):
        cols = slice(256 * n, 256 * n + 256)
        m5[:, cols] = dot(lyi[...], m4[:, cols])

    sums = []
    for part in range(2):
        vals = []
        for a in range(8):
            cols = slice((8 * part + a) * 128, (8 * part + a) * 128 + 128)
            vals += swap_chunks([m5[8 * j:8 * j + 8, cols] for j in range(4)], odd1, odd2)
        sums.append(combine(trig[32 * part:32 * part + 32, 16:32].T, vals))
    for n in range(16):
        for x, val in ((16 + n, sums[0][n] + sums[1][n]), (15 - n, sums[0][n] - sums[1][n])):
            pbuf[pl.ds(16 * (x // 2) + x % 2, 8, stride=2), :] = val

    slot = (1 - half) * 16 + r

    def send_potential(i, _):
        p = lax.rem(me + i, 32)
        rows = pl.multiple_of(16 * lax.rem(p, 16) + 8 * (p // 16), 8)
        pltpu.make_async_remote_copy(
            pbuf.at[pl.ds(rows, 8)], pl_in.at[slot], a2_send, a2_recv,
            device_id=(base + p // 16, lax.rem(p, 16)), device_id_type=MESH,
        ).start()
        return 0

    lax.fori_loop(1, 32, send_potential, 0)
    keep = pltpu.make_async_copy(
        pbuf.at[pl.ds(pl.multiple_of(16 * r + 8 * half, 8), 8)], pl_in.at[slot], a2_loc
    )
    keep.start()

    def prepare(d):
        for rho in range(8):
            hi, lo = split(vl[32 * d:32 * d + 32, rho, :])
            vh[32 * d:32 * d + 32, 128 * rho:128 * rho + 128] = hi
            vlo[32 * d:32 * d + 32, 128 * rho:128 * rho + 128] = lo

    own.wait()
    wait_part(0, 1 - half, 0)
    prepare(0)
    prepare(1)
    relay(3)
    prepare(2)
    prepare(3)
    relay(4)
    prepare(4)

    keep.wait()
    rest = pl_in.at[pl.ds(0, 31)]
    pltpu.make_async_copy(rest, rest, a2_recv).wait()
    parts = [split(pl_in[:, rho, :]) for rho in range(8)]
    ph = jnp.concatenate([p[0] for p in parts], axis=1)
    plo = jnp.concatenate([p[1] for p in parts], axis=1)
    gram = dot_nt(ph, vh[...]) + dot_nt(plo, vh[...]) + dot_nt(ph, vlo[...])
    pad = jnp.zeros((16, 112), F32)
    sb[0:16, 0, :] = gram[0:16, 0:128]
    sb[0:16, 1, :] = jnp.concatenate([gram[0:16, 128:144], pad], axis=1)
    sb[16:32, 0, :] = gram[16:32, 16:144]
    sb[16:32, 1, :] = jnp.concatenate([gram[16:32, 144:160], pad], axis=1)

    def send_sum(i, _):
        p = lax.rem(me + i, 32)
        pltpu.make_async_remote_copy(
            sb.at[p], rl.at[me], r_send, r_recv,
            device_id=(base + p // 16, lax.rem(p, 16)), device_id_type=MESH,
        ).start()
        return 0

    lax.fori_loop(1, 32, send_sum, 0)
    keep = pltpu.make_async_copy(sb.at[me], rl.at[me], r_loc)
    keep.start()
    keep.wait()
    rest = rl.at[pl.ds(0, 31)]
    pltpu.make_async_copy(rest, rest, r_recv).wait()
    total = rl[0]
    for i in range(1, 32):
        total = total + rl[i]
    for s in range(9):
        out_ref[0, s:s + 1, :] = total[s // 8:s // 8 + 1, 16 * (s % 8):16 * (s % 8) + 16]

    for c in first:
        c.wait_send()
    for d in range(1, REACH):
        for k in range(2):
            part = half if k == 0 else 1 - half
            move(vl.at[pl.ds(32 * d + 16 * part, 16)], d + 1, part, 2 * d + 1 + k, down).wait_send()
    pltpu.make_async_copy(u, u, a1_send).wait()
    rest = pl_in.at[pl.ds(0, 31)]
    pltpu.make_async_copy(rest, rest, a2_send).wait()
    rest = rl.at[pl.ds(0, 31)]
    pltpu.make_async_copy(rest, rest, r_send).wait()


def body(fitting_vectors):
    ly, lyi, bz, bzi, kt, trig = constants()
    rows = fitting_vectors.reshape(16, 2, 8, 128).transpose(0, 2, 1, 3).reshape(16, 16, 128)
    any_spec = pl.BlockSpec(memory_space=pl.ANY)
    dma = pltpu.SemaphoreType.DMA
    return pl.pallas_call(
        functools.partial(body_kernel, trig),
        name="coulomb",
        out_shape=jax.ShapeDtypeStruct((1, 9, 16), F32),
        in_specs=[any_spec] * 6,
        out_specs=pl.BlockSpec(memory_space=pltpu.VMEM),
        scratch_shapes=[
            pltpu.VMEM((256, 128), F32),
            pltpu.VMEM((256, 128), F32),
            pltpu.VMEM((32, 8, 128), F32),
            pltpu.VMEM((160, 8, 128), F32),
            pltpu.VMEM(ly.shape, BF16),
            pltpu.VMEM(lyi.shape, BF16),
            pltpu.VMEM(bz.shape, BF16),
            pltpu.VMEM(bzi.shape, BF16),
            pltpu.VMEM(kt.shape, F32),
            pltpu.VMEM((96, 2048), BF16),
            pltpu.VMEM((512, 256), BF16),
            pltpu.VMEM((512, 256), BF16),
            pltpu.VMEM((512, 512), BF16),
            pltpu.VMEM((512, 512), BF16),
            pltpu.VMEM((192, 2048), BF16),
            pltpu.VMEM((32, 2048), F32),
            pltpu.VMEM((160, 1024), BF16),
            pltpu.VMEM((160, 1024), BF16),
            pltpu.VMEM((32, 2, 128), F32),
            pltpu.VMEM((32, 2, 128), F32),
            dma((5,)),
            dma, dma,
            dma((9,)), dma((9,)), dma,
            dma, dma, dma,
            dma, dma, dma,
        ],
        compiler_params=pltpu.CompilerParams(collective_id=0, has_side_effects=True),
    )(rows, ly, lyi, bz, bzi, kt)


def solution(mesh):
    return jax.shard_map(
        body,
        mesh=mesh,
        in_specs=(P("vec", "grid", None),),
        out_specs=P(("vec", "grid"), None, None),
        check_vma=False,
    )
```

profile of v0, /device:TPU:1, one launch (start us, length us, event | category | flops | bytes accessed | tf_op | source)
XLA Modules:
  0.0 36.3 jit_solution(17331675269220084572)
XLA Ops:
  0.0 35.0 %coulomb.1 = f32[1,9,16]{2,1,0:T(8,128)} custom-call(f32[16,16,128]{2,1,0:T(8,128)} %bitcast.5, bf16[64,96]{1,0:T(8,128)(2,1)} %constant.10.clone.ly_in, bf16[32,192]{1,0:T(8,128)(2,1)} %constant.11.clone.lyi_in, bf16[2,256,512]{2,1,0:T(8,128)(2,1)} %constant.12.clone.bz_in, bf16[256,256]{1,0:T(8,128)(2,1)} %constant.13.clone.bzi_in, ...), custom_call_target="tpu_custom_call" | custom-call | tf_op jit(solution)/shard_map/coulomb/pallas_call | solution.py:336
  35.0 1.3 %copy.8 = f32[1,9,16]{2,0,1:T(1,128)} copy(f32[1,9,16]{2,1,0:T(8,128)} %coulomb.1) | data formatting | bytes 1152 | tf_op jit(solution)/shard_map/coulomb/pallas_call | solution.py:336
where the time goes:
time: 36.4 us; the launch traced here: 36.3 us
  Pallas kernels  35 us (96%)
  local copies, waits for them, and re-layouts  1.29 us (4%)
    pallas_call x1, Pallas kernels, body(): pl.pallas_call(functools.partial(body_kernel, trig), name='coulomb', out_...  35 us
    pallas_call x1, local copies, waits for them, and re-layouts, body(): pl.pallas_call(functools.partial(body_kernel, trig), name='coulomb', out_...  1.29 us

commit v1 on v0

--- a/solution.py
+++ b/solution.py
@@ -15,6 +15,8 @@
 BF16 = jnp.bfloat16
 MESH = pl.DeviceIdType.MESH
 REACH = 4
+PIECES = 2
+STEP = 16 // PIECES
 
 
 def tables():
@@ -114,8 +116,17 @@
     down_sib = lax.rem(sib + 14, 16)
     up = lax.rem(g + 2, 16)
     up_sib = lax.rem(sib + 2, 16)
-    base = g - half
-    me = half * 16 + r
+
+    me = 16 * half + r
+
+    def turn(i):
+        return lax.rem(r + i, 16)
+
+    def others():
+        for i in range(16):
+            yield sib, 1 - half, turn(i)
+            if i:
+                yield g, half, turn(i)
 
     consts = [
         pltpu.make_async_copy(a, b, c_sem.at[i])
@@ -124,62 +135,65 @@
     for c in consts:
         c.start()
     own = pltpu.make_async_copy(
-        v_in.at[:, pl.ds(8 * half, 8), :], vl.at[pl.ds(16 * half, 16)], v_loc
+        v_in.at[:, pl.ds(pl.multiple_of(8 * half, 8), 8), :], vl.at[pl.ds(16 * half, 16)], v_loc
     )
     own.start()
 
     barrier = pltpu.get_barrier_semaphore()
 
-    def greet(i, _):
-        p = lax.rem(me + i, 32)
-        pl.semaphore_signal(
-            barrier, inc=1, device_id=(base + p // 16, lax.rem(p, 16)), device_id_type=MESH
-        )
-        return 0
-
-    lax.fori_loop(1, 32, greet, 0)
-    for other in (down, down_sib, up, up_sib):
-        pl.semaphore_signal(barrier, inc=1, device_id=(other, r), device_id_type=MESH)
-    pl.semaphore_wait(barrier, 35)
-
-    def send_slab(m, _):
+    for i in range(16):
+        pl.semaphore_signal(barrier, inc=1, device_id=(sib, turn(i)), device_id_type=MESH)
+    for peer in (down, down_sib, up, up_sib):
+        pl.semaphore_signal(barrier, inc=1, device_id=(peer, r), device_id_type=MESH)
+    pl.semaphore_wait(barrier, 20)
+
+    for i in range(16):
+        m = turn(i)
         pltpu.make_async_remote_copy(
-            v_in.at[m], u.at[pl.ds(16 * r, 16)], a1_send, a1_recv,
+            v_in.at[m], u.at[pl.ds(pl.multiple_of(16 * r, 16), 16)], a1_send, a1_recv,
             device_id=(sib, m), device_id_type=MESH,
         ).start()
-        return 0
-
-    lax.fori_loop(0, 16, send_slab, 0)
-
-    def move(src, d, part, sem, target):
+
+    def block(d, part, k):
+        return vl.at[pl.ds(pl.multiple_of(32 * d + 16 * part + STEP * k, STEP), STEP)]
+
+    def sem_of(d, far, k):
+        return (2 * d + far) * PIECES + k
+
+    def move(src, d, far, part, k, target):
         return pltpu.make_async_remote_copy(
-            src, vl.at[pl.ds(32 * d + 16 * part, 16)], v_send.at[sem], v_recv.at[sem],
+            src, block(d, part, k), v_send.at[sem_of(d, far, k)], v_recv.at[sem_of(d, far, k)],
             device_id=(target, r), device_id_type=MESH,
         )
 
-    mine = v_in.at[:, pl.ds(8 * half, 8), :]
-    other = v_in.at[:, pl.ds(8 * (1 - half), 8), :]
-    first = [
-        move(mine, 1, half, 1, down),
-        move(other, 1, half, 2, down_sib),
-        move(other, 0, half, 0, sib),
-    ]
+    def source(h, k):
+        return v_in.at[pl.ds(STEP * k, STEP), pl.ds(pl.multiple_of(8 * h, 8), 8), :]
+
+    first = [move(source(half, k), 1, 0, half, k, down) for k in range(PIECES)]
+    first += [move(source(1 - half, k), 1, 1, half, k, down_sib) for k in range(PIECES)]
+    first += [move(source(1 - half, k), 0, 1, half, k, sib) for k in range(PIECES)]
     for c in first:
         c.start()
 
-    def wait_part(d, part, sem):
-        ref = vl.at[pl.ds(32 * d + 16 * part, 16)]
-        pltpu.make_async_copy(ref, ref, v_recv.at[sem]).wait()
-
-    def relay(d):
-        for k in range(2):
-            part = half if k == 0 else 1 - half
-            wait_part(d, part, 2 * d - 1 + k)
+    def part_of(far):
+        return 1 - half if far else half
+
+    def wait_block(d, far, k):
+        ref = block(d, part_of(far), k)
+        pltpu.make_async_copy(ref, ref, v_recv.at[sem_of(d, far, k)]).wait()
+
+    def onward(d, far, k):
+        return move(block(d, part_of(far), k), d + 1, far, part_of(far), k, down)
+
+    def relay(d, far):
+        for k in range(PIECES):
+            wait_block(d, far, k)
             if d < REACH:
-                ref = vl.at[pl.ds(32 * d + 16 * part, 16)]
-                move(ref, d + 1, part, 2 * d + 1 + k, down).start()
-
-    relay(1)
+                onward(d, far, k).start()
+
+    relay(1, 0)
+    relay(1, 1)
+    relay(2, 0)
     for c in consts:
         c.wait()
     pltpu.make_async_copy(u, u, a1_recv).wait()
@@ -220,7 +234,8 @@
         m3h[rows, :] = hi
         m3l[rows, :] = lo
 
-    relay(2)
+    relay(2, 1)
+    relay(3, 0)
 
     for n in range(8):
         rows = slice(64 * n, 64 * n + 64)
@@ -251,16 +266,12 @@
 
     slot = (1 - half) * 16 + r
 
-    def send_potential(i, _):
-        p = lax.rem(me + i, 32)
-        rows = pl.multiple_of(16 * lax.rem(p, 16) + 8 * (p // 16), 8)
+    for vec, h, m in others():
+        rows = pl.multiple_of(16 * m + 8 * h, 8)
         pltpu.make_async_remote_copy(
             pbuf.at[pl.ds(rows, 8)], pl_in.at[slot], a2_send, a2_recv,
-            device_id=(base + p // 16, lax.rem(p, 16)), device_id_type=MESH,
+            device_id=(vec, m), device_id_type=MESH,
         ).start()
-        return 0
-
-    lax.fori_loop(1, 32, send_potential, 0)
     keep = pltpu.make_async_copy(
         pbuf.at[pl.ds(pl.multiple_of(16 * r + 8 * half, 8), 8)], pl_in.at[slot], a2_loc
     )
@@ -272,15 +283,15 @@
             vh[32 * d:32 * d + 32, 128 * rho:128 * rho + 128] = hi
             vlo[32 * d:32 * d + 32, 128 * rho:128 * rho + 128] = lo
 
+    relay(3, 1)
     own.wait()
-    wait_part(0, 1 - half, 0)
-    prepare(0)
-    prepare(1)
-    relay(3)
-    prepare(2)
-    prepare(3)
-    relay(4)
-    prepare(4)
+    for k in range(PIECES):
+        wait_block(0, 1, k)
+    for d in range(REACH):
+        prepare(d)
+    relay(REACH, 0)
+    relay(REACH, 1)
+    prepare(REACH)
 
     keep.wait()
     rest = pl_in.at[pl.ds(0, 31)]
@@ -295,15 +306,10 @@
     sb[16:32, 0, :] = gram[16:32, 16:144]
     sb[16:32, 1, :] = jnp.concatenate([gram[16:32, 144:160], pad], axis=1)
 
-    def send_sum(i, _):
-        p = lax.rem(me + i, 32)
+    for vec, h, m in others():
         pltpu.make_async_remote_copy(
-            sb.at[p], rl.at[me], r_send, r_recv,
-            device_id=(base + p // 16, lax.rem(p, 16)), device_id_type=MESH,
+            sb.at[16 * h + m], rl.at[me], r_send, r_recv, device_id=(vec, m), device_id_type=MESH
         ).start()
-        return 0
-
-    lax.fori_loop(1, 32, send_sum, 0)
     keep = pltpu.make_async_copy(sb.at[me], rl.at[me], r_loc)
     keep.start()
     keep.wait()
@@ -313,14 +319,14 @@
     for i in range(1, 32):
         total = total + rl[i]
     for s in range(9):
-        out_ref[0, s:s + 1, :] = total[s // 8:s // 8 + 1, 16 * (s % 8):16 * (s % 8) + 16]
+        out_ref[s] = total[s // 8:s // 8 + 1, 16 * (s % 8):16 * (s % 8) + 16]
 
     for c in first:
         c.wait_send()
     for d in range(1, REACH):
-        for k in range(2):
-            part = half if k == 0 else 1 - half
-            move(vl.at[pl.ds(32 * d + 16 * part, 16)], d + 1, part, 2 * d + 1 + k, down).wait_send()
+        for far in range(2):
+            for k in range(PIECES):
+                onward(d, far, k).wait_send()
     pltpu.make_async_copy(u, u, a1_send).wait()
     rest = pl_in.at[pl.ds(0, 31)]
     pltpu.make_async_copy(rest, rest, a2_send).wait()
@@ -333,10 +339,10 @@
     rows = fitting_vectors.reshape(16, 2, 8, 128).transpose(0, 2, 1, 3).reshape(16, 16, 128)
     any_spec = pl.BlockSpec(memory_space=pl.ANY)
     dma = pltpu.SemaphoreType.DMA
-    return pl.pallas_call(
+    out = pl.pallas_call(
         functools.partial(body_kernel, trig),
         name="coulomb",
-        out_shape=jax.ShapeDtypeStruct((1, 9, 16), F32),
+        out_shape=jax.ShapeDtypeStruct((9, 1, 16), F32),
         in_specs=[any_spec] * 6,
         out_specs=pl.BlockSpec(memory_space=pltpu.VMEM),
         scratch_shapes=[
@@ -362,12 +368,13 @@
             pltpu.VMEM((32, 2, 128), F32),
             dma((5,)),
             dma, dma,
-            dma((9,)), dma((9,)), dma,
+            dma((10 * PIECES,)), dma((10 * PIECES,)), dma,
             dma, dma, dma,
             dma, dma, dma,
         ],
         compiler_params=pltpu.CompilerParams(collective_id=0, has_side_effects=True),
     )(rows, ly, lyi, bz, bzi, kt)
+    return out.transpose(1, 0, 2)
 
 
 def solution(mesh):

time: 36.4 us -> 34.3 us (0.942)
  the two profiles are of different devices: /device:TPU:1 before, /device:TPU:33 now
where the time goes in v1:
time: 34.3 us; the launch traced here: 34.2 us
  Pallas kernels  32.9 us (96%)
  local copies, waits for them, and re-layouts  1.28 us (4%)
    pallas_call x1, Pallas kernels, body(): pl.pallas_call(functools.partial(body_kernel, trig), name='coulomb', out_...  32.9 us
    unnamed x1, local copies, waits for them, and re-layouts  1.28 us

profile of v1, /device:TPU:33, one launch (start us, length us, event | category | flops | bytes accessed | tf_op | source)
XLA Modules:
  0.0 34.2 jit_solution(856066343808311059)
XLA Ops:
  0.0 32.9 %coulomb.1 = f32[9,1,16]{2,1,0:T(1,128)} custom-call(f32[16,16,128]{2,1,0:T(8,128)} %bitcast.6, bf16[64,96]{1,0:T(8,128)(2,1)} %constant.10.clone.ly_in, bf16[32,192]{1,0:T(8,128)(2,1)} %constant.11.clone.lyi_in, bf16[2,256,512]{2,1,0:T(8,128)(2,1)} %constant.12.clone.bz_in, bf16[256,256]{1,0:T(8,128)(2,1)} %constant.13.clone.bzi_in, ...), custom_call_target="tpu_custom_call" | custom-call | tf_op jit(solution)/shard_map/coulomb/pallas_call | solution.py:342
  32.9 1.3 %copy.9 = f32[1,9,16]{2,0,1:T(1,128)} copy(f32[1,9,16]{2,0,1:T(1,128)} %bitcast.7) | data formatting | bytes 1152

commit v2 on v1

--- a/solution.py
+++ b/solution.py
@@ -17,6 +17,8 @@
 REACH = 4
 PIECES = 2
 STEP = 16 // PIECES
+BEFORE = 8
+MIDDLE = 8
 
 
 def tables():
@@ -145,7 +147,13 @@
         pl.semaphore_signal(barrier, inc=1, device_id=(sib, turn(i)), device_id_type=MESH)
     for peer in (down, down_sib, up, up_sib):
         pl.semaphore_signal(barrier, inc=1, device_id=(peer, r), device_id_type=MESH)
-    pl.semaphore_wait(barrier, 20)
+    @pl.when(g < 2)
+    def _():
+        for peer in (g, sib):
+            pl.semaphore_signal(barrier, inc=1, device_id=(peer + 8, r), device_id_type=MESH)
+
+    early = jnp.where(jnp.logical_and(g >= 8, g < 10), 2, 0)
+    pl.semaphore_wait(barrier, 20 + early)
 
     for i in range(16):
         m = turn(i)
@@ -160,19 +168,37 @@
     def sem_of(d, far, k):
         return (2 * d + far) * PIECES + k
 
-    def move(src, d, far, part, k, target):
+    def move(src, d, far, part, k, target, leave=0):
         return pltpu.make_async_remote_copy(
-            src, block(d, part, k), v_send.at[sem_of(d, far, k)], v_recv.at[sem_of(d, far, k)],
+            src, block(d, part, k), v_send.at[sem_of(d + leave, far, k)], v_recv.at[sem_of(d, far, k)],
             device_id=(target, r), device_id_type=MESH,
         )
 
     def source(h, k):
         return v_in.at[pl.ds(STEP * k, STEP), pl.ds(pl.multiple_of(8 * h, 8), 8), :]
 
-    first = [move(source(half, k), 1, 0, half, k, down) for k in range(PIECES)]
-    first += [move(source(1 - half, k), 1, 1, half, k, down_sib) for k in range(PIECES)]
+    first = []
+    for k in range(PIECES):
+        first.append(move(source(half, k), 1, 0, half, k, down))
+        first.append(move(source(1 - half, k), 1, 1, half, k, down_sib))
     first += [move(source(1 - half, k), 0, 1, half, k, sib) for k in range(PIECES)]
-    for c in first:
+    plane = g // 2
+    late = jnp.logical_and(plane >= 4, plane <= 4)
+    passes = jnp.logical_or(plane < 1, plane > 1)
+    direct = []
+    for k in range(PIECES):
+        direct.append(move(source(half, k), REACH, 0, half, k, lax.rem(g + 8, 16), 1))
+        direct.append(move(source(1 - half, k), REACH, 1, half, k, lax.rem(sib + 8, 16), 1))
+
+    for c in first[:2 * PIECES]:
+        c.start()
+
+    @pl.when(late)
+    def _():
+        for c in direct:
+            c.start()
+
+    for c in first[2 * PIECES:]:
         c.start()
 
     def part_of(far):
@@ -185,15 +211,18 @@
     def onward(d, far, k):
         return move(block(d, part_of(far), k), d + 1, far, part_of(far), k, down)
 
-    def relay(d, far):
-        for k in range(PIECES):
-            wait_block(d, far, k)
-            if d < REACH:
-                onward(d, far, k).start()
-
-    relay(1, 0)
-    relay(1, 1)
-    relay(2, 0)
+    hops = iter([(d, far, k) for d in range(1, REACH) for k in range(PIECES) for far in range(2)])
+
+    def relay(count):
+        for _ in range(count * 2 * PIECES // 8):
+            hop = next(hops)
+            wait_block(*hop)
+            if hop[0] < REACH - 1:
+                onward(*hop).start()
+            else:
+                pl.when(passes)(onward(*hop).start)
+
+    relay(BEFORE)
     for c in consts:
         c.wait()
     pltpu.make_async_copy(u, u, a1_recv).wait()
@@ -202,11 +231,11 @@
     odd1 = lane % 2 == 1
     odd2 = lane >= 2
 
-    def plane(x):
+    def slice_at(x):
         return u[pl.ds(16 * (x // 2) + x % 2, 8, stride=2), :]
 
-    low = [plane(15 - n) for n in range(16)]
-    high = [plane(16 + n) for n in range(16)]
+    low = [slice_at(15 - n) for n in range(16)]
+    high = [slice_at(16 + n) for n in range(16)]
     for part in range(2):
         if part == 0:
             vals = [a + b for a, b in zip(high, low)]
@@ -234,8 +263,7 @@
         m3h[rows, :] = hi
         m3l[rows, :] = lo
 
-    relay(2, 1)
-    relay(3, 0)
+    relay(MIDDLE)
 
     for n in range(8):
         rows = slice(64 * n, 64 * n + 64)
@@ -283,14 +311,15 @@
             vh[32 * d:32 * d + 32, 128 * rho:128 * rho + 128] = hi
             vlo[32 * d:32 * d + 32, 128 * rho:128 * rho + 128] = lo
 
-    relay(3, 1)
+    relay(24 - BEFORE - MIDDLE)
     own.wait()
     for k in range(PIECES):
         wait_block(0, 1, k)
     for d in range(REACH):
         prepare(d)
-    relay(REACH, 0)
-    relay(REACH, 1)
+    for k in range(PIECES):
+        wait_block(REACH, 0, k)
+        wait_block(REACH, 1, k)
     prepare(REACH)
 
     keep.wait()
@@ -323,10 +352,19 @@
 
     for c in first:
         c.wait_send()
+
+    @pl.when(late)
+    def _():
+        for c in direct:
+            c.wait_send()
+
     for d in range(1, REACH):
         for far in range(2):
             for k in range(PIECES):
-                onward(d, far, k).wait_send()
+                if d < REACH - 1:
+                    onward(d, far, k).wait_send()
+                else:
+                    pl.when(passes)(onward(d, far, k).wait_send)
     pltpu.make_async_copy(u, u, a1_send).wait()
     rest = pl_in.at[pl.ds(0, 31)]
     pltpu.make_async_copy(rest, rest, a2_send).wait()
@@ -368,7 +406,7 @@
             pltpu.VMEM((32, 2, 128), F32),
             dma((5,)),
             dma, dma,
-            dma((10 * PIECES,)), dma((10 * PIECES,)), dma,
+            dma((12 * PIECES,)), dma((10 * PIECES,)), dma,
             dma, dma, dma,
             dma, dma, dma,
         ],

time: 34.3 us -> 32.4 us (0.945)
  Pallas kernels: 32.9 us -> 30.8 us
    pallas_call x1, Pallas kernels: 32.9 us -> 30.8 us  [body(): pl.pallas_call(functools.partial(body_kernel, trig), name='coulomb', out_...]
where the time goes in v2:
time: 32.4 us; the launch traced here: 32.1 us
  Pallas kernels  30.8 us (95%)
  local copies, waits for them, and re-layouts  1.28 us (4%)
    pallas_call x1, Pallas kernels, body(): pl.pallas_call(functools.partial(body_kernel, trig), name='coulomb', out_...  30.8 us
    unnamed x1, local copies, waits for them, and re-layouts  1.28 us

profile of v2, /device:TPU:33, one launch (start us, length us, event | category | flops | bytes accessed | tf_op | source)
XLA Modules:
  0.0 32.1 jit_solution(13147485900982647327)
XLA Ops:
  0.0 30.8 %coulomb.1 = f32[9,1,16]{2,1,0:T(1,128)} custom-call(f32[16,16,128]{2,1,0:T(8,128)} %bitcast.6, bf16[64,96]{1,0:T(8,128)(2,1)} %constant.10.clone.ly_in, bf16[32,192]{1,0:T(8,128)(2,1)} %constant.11.clone.lyi_in, bf16[2,256,512]{2,1,0:T(8,128)(2,1)} %constant.12.clone.bz_in, bf16[256,256]{1,0:T(8,128)(2,1)} %constant.13.clone.bzi_in, ...), custom_call_target="tpu_custom_call" | custom-call | tf_op jit(solution)/shard_map/coulomb/pallas_call | solution.py:380
  30.8 1.3 %copy.9 = f32[1,9,16]{2,0,1:T(1,128)} copy(f32[1,9,16]{2,0,1:T(1,128)} %bitcast.7) | data formatting | bytes 1152

commit v3 on v2

--- a/solution.py
+++ b/solution.py
@@ -15,10 +15,10 @@
 BF16 = jnp.bfloat16
 MESH = pl.DeviceIdType.MESH
 REACH = 4
-PIECES = 2
+PIECES = 4
 STEP = 16 // PIECES
-BEFORE = 8
-MIDDLE = 8
+BEFORE = 12
+MIDDLE = 4
 
 
 def tables():
@@ -105,10 +105,10 @@
 def body_kernel(
     trig,
     v_in, ly_in, lyi_in, bz_in, bzi_in, kt_in,
-    out_ref,
+    rl,
     u, pbuf, pl_in, vl, ly, lyi, bz, bzi, kt,
-    m1, m2h, m2l, m3h, m3l, m4, m5, vh, vlo, sb, rl,
-    c_sem, a1_send, a1_recv, v_send, v_recv, v_loc, a2_send, a2_recv, a2_loc, r_send, r_recv, r_loc,
+    m1, m2h, m2l, m3h, m3l, m4, m5, vh, vlo, sb,
+    ready, ready_up, c_sem, a1_send, a1_recv, v_send, v_recv, v_loc, a2_send, a2_recv, a2_loc, r_send, r_recv, r_loc,
 ):
     g = lax.axis_index("vec")
     r = lax.axis_index("grid")
@@ -129,6 +129,37 @@
             yield sib, 1 - half, turn(i)
             if i:
                 yield g, half, turn(i)
+
+    plane = g // 2
+    barrier = pltpu.get_barrier_semaphore()
+
+    def rank(x, y_hi, parity):
+        return 2 * (jnp.minimum(x, 2) + jnp.minimum(2 * y_hi + parity, 2)) + parity
+
+    my_rank = rank(r // 4, lax.rem(r, 4) // 2, half)
+    later = [
+        (m, (rank(m // 4, m % 4 // 2, 1 - half) > my_rank).astype(jnp.int32)) for m in range(16)
+    ]
+    n_later = functools.reduce(lambda a, b: a + b, [after for _, after in later])
+
+    def greet(sem, vec, to):
+        pl.semaphore_signal(sem, inc=1, device_id=(vec, to), device_id_type=MESH)
+
+    greet(barrier, g, r + 1 - 2 * lax.rem(r, 2))
+
+    @pl.when(plane < 7)
+    def _():
+        greet(barrier, up, r)
+        greet(barrier, up_sib, r)
+
+    for m, after in later:
+        pl.when(after == 1)(functools.partial(greet, barrier, sib, m))
+
+    @pl.when(plane == 0)
+    def _():
+        for away in (8, 14):
+            greet(barrier, g + away, r)
+            greet(barrier, sib + away, r)
 
     consts = [
         pltpu.make_async_copy(a, b, c_sem.at[i])
@@ -141,19 +172,55 @@
     )
     own.start()
 
-    barrier = pltpu.get_barrier_semaphore()
-
-    for i in range(16):
-        pl.semaphore_signal(barrier, inc=1, device_id=(sib, turn(i)), device_id_type=MESH)
-    for peer in (down, down_sib, up, up_sib):
-        pl.semaphore_signal(barrier, inc=1, device_id=(peer, r), device_id_type=MESH)
-    @pl.when(g < 2)
-    def _():
-        for peer in (g, sib):
-            pl.semaphore_signal(barrier, inc=1, device_id=(peer + 8, r), device_id_type=MESH)
-
-    early = jnp.where(jnp.logical_and(g >= 8, g < 10), 2, 0)
-    pl.semaphore_wait(barrier, 20 + early)
+    across = jnp.where(plane > 0, 2, 0) + jnp.where(jnp.logical_or(plane == 4, plane == 7), 2, 0)
+    pl.semaphore_wait(barrier, 17 - n_later + across)
+
+    for m, after in later:
+        pl.when(after == 0)(functools.partial(greet, ready, sib, m))
+
+    @pl.when(plane == 7)
+    def _():
+        greet(ready_up, up, r)
+        greet(ready_up, up_sib, r)
+
+    def block(d, part, k):
+        return vl.at[pl.ds(pl.multiple_of(32 * d + 16 * part + STEP * k, STEP), STEP)]
+
+    def sem_of(d, far, k):
+        return (2 * d + far) * PIECES + k
+
+    def move(src, d, far, part, k, target, leave=0):
+        return pltpu.make_async_remote_copy(
+            src, block(d, part, k), v_send.at[sem_of(d + leave, far, k)], v_recv.at[sem_of(d, far, k)],
+            device_id=(target, r), device_id_type=MESH,
+        )
+
+    def source(h, k):
+        return v_in.at[pl.ds(STEP * k, STEP), pl.ds(pl.multiple_of(8 * h, 8), 8), :]
+
+    first = []
+    for k in range(PIECES):
+        first.append(move(source(half, k), 1, 0, half, k, down))
+        first.append(move(source(1 - half, k), 1, 1, half, k, down_sib))
+    first += [move(source(1 - half, k), 0, 1, half, k, sib) for k in range(PIECES)]
+    passes = plane != 1
+    direct = []
+    for k in range(PIECES):
+        direct.append(move(source(half, k), REACH, 0, half, k, lax.rem(g + 8, 16), 1))
+        direct.append(move(source(1 - half, k), REACH, 1, half, k, lax.rem(sib + 8, 16), 1))
+
+    def start_down():
+        for c in first[:2 * PIECES]:
+            c.start()
+
+    pl.when(plane > 0)(start_down)
+
+    @pl.when(plane == 4)
+    def _():
+        for c in direct:
+            c.start()
+
+    pl.when(n_later > 0)(lambda: pl.semaphore_wait(ready, n_later))
 
     for i in range(16):
         m = turn(i)
@@ -162,44 +229,13 @@
             device_id=(sib, m), device_id_type=MESH,
         ).start()
 
-    def block(d, part, k):
-        return vl.at[pl.ds(pl.multiple_of(32 * d + 16 * part + STEP * k, STEP), STEP)]
-
-    def sem_of(d, far, k):
-        return (2 * d + far) * PIECES + k
-
-    def move(src, d, far, part, k, target, leave=0):
-        return pltpu.make_async_remote_copy(
-            src, block(d, part, k), v_send.at[sem_of(d + leave, far, k)], v_recv.at[sem_of(d, far, k)],
-            device_id=(target, r), device_id_type=MESH,
-        )
-
-    def source(h, k):
-        return v_in.at[pl.ds(STEP * k, STEP), pl.ds(pl.multiple_of(8 * h, 8), 8), :]
-
-    first = []
-    for k in range(PIECES):
-        first.append(move(source(half, k), 1, 0, half, k, down))
-        first.append(move(source(1 - half, k), 1, 1, half, k, down_sib))
-    first += [move(source(1 - half, k), 0, 1, half, k, sib) for k in range(PIECES)]
-    plane = g // 2
-    late = jnp.logical_and(plane >= 4, plane <= 4)
-    passes = jnp.logical_or(plane < 1, plane > 1)
-    direct = []
-    for k in range(PIECES):
-        direct.append(move(source(half, k), REACH, 0, half, k, lax.rem(g + 8, 16), 1))
-        direct.append(move(source(1 - half, k), REACH, 1, half, k, lax.rem(sib + 8, 16), 1))
-
-    for c in first[:2 * PIECES]:
-        c.start()
-
-    @pl.when(late)
-    def _():
-        for c in direct:
-            c.start()
-
     for c in first[2 * PIECES:]:
         c.start()
+
+    @pl.when(plane == 0)
+    def _():
+        pl.semaphore_wait(ready_up, 2)
+        start_down()
 
     def part_of(far):
         return 1 - half if far else half
@@ -344,16 +380,10 @@
     keep.wait()
     rest = rl.at[pl.ds(0, 31)]
     pltpu.make_async_copy(rest, rest, r_recv).wait()
-    total = rl[0]
-    for i in range(1, 32):
-        total = total + rl[i]
-    for s in range(9):
-        out_ref[s] = total[s // 8:s // 8 + 1, 16 * (s % 8):16 * (s % 8) + 16]
-
     for c in first:
         c.wait_send()
 
-    @pl.when(late)
+    @pl.when(plane == 4)
     def _():
         for c in direct:
             c.wait_send()
@@ -372,17 +402,23 @@
     pltpu.make_async_copy(rest, rest, r_send).wait()
 
 
+def finish(parts, out):
+    total = jnp.sum(parts[...], axis=0)
+    for s in range(9):
+        out[s] = total[s // 8:s // 8 + 1, 16 * (s % 8):16 * (s % 8) + 16]
+
+
 def body(fitting_vectors):
     ly, lyi, bz, bzi, kt, trig = constants()
     rows = fitting_vectors.reshape(16, 2, 8, 128).transpose(0, 2, 1, 3).reshape(16, 16, 128)
     any_spec = pl.BlockSpec(memory_space=pl.ANY)
     dma = pltpu.SemaphoreType.DMA
-    out = pl.pallas_call(
+    partial = pl.pallas_call(
         functools.partial(body_kernel, trig),
         name="coulomb",
-        out_shape=jax.ShapeDtypeStruct((9, 1, 16), F32),
+        out_shape=jax.ShapeDtypeStruct((32, 2, 128), F32),
         in_specs=[any_spec] * 6,
-        out_specs=pl.BlockSpec(memory_space=pltpu.VMEM),
+        out_specs=any_spec,
         scratch_shapes=[
             pltpu.VMEM((256, 128), F32),
             pltpu.VMEM((256, 128), F32),
@@ -403,7 +439,8 @@
             pltpu.VMEM((160, 1024), BF16),
             pltpu.VMEM((160, 1024), BF16),
             pltpu.VMEM((32, 2, 128), F32),
-            pltpu.VMEM((32, 2, 128), F32),
+            pltpu.SemaphoreType.REGULAR,
+            pltpu.SemaphoreType.REGULAR,
             dma((5,)),
             dma, dma,
             dma((12 * PIECES,)), dma((10 * PIECES,)), dma,
@@ -412,6 +449,13 @@
         ],
         compiler_params=pltpu.CompilerParams(collective_id=0, has_side_effects=True),
     )(rows, ly, lyi, bz, bzi, kt)
+    out = pl.pallas_call(
+        finish,
+        name="finish",
+        out_shape=jax.ShapeDtypeStruct((9, 1, 16), F32),
+        in_specs=[pl.BlockSpec(memory_space=pltpu.VMEM)],
+        out_specs=pl.BlockSpec(memory_space=pltpu.VMEM),
+    )(partial)
     return out.transpose(1, 0, 2)
 
 

time: 32.4 us -> 31.6 us (0.975)
  local copies, waits for them, and re-layouts: 1.28 us -> 0 us
  Pallas kernels: 30.8 us -> 31.4 us
    pallas_call x0 -> x1, Pallas kernels: none -> 1.46 us  [body(): pl.pallas_call(finish, name='finish', out_shape=jax.ShapeDtypeStruct((9,...]
    unnamed x1 -> x0, local copies, waits for them, and re-layouts: 1.28 us -> none
    pallas_call x1, Pallas kernels: 30.8 us -> 30 us  [body(): pl.pallas_call(functools.partial(body_kernel, trig), name='coulomb', out_...]
where the time goes in v3:
time: 31.6 us; the launch traced here: 31.5 us
  Pallas kernels  31.4 us (99%)
    pallas_call x1, Pallas kernels, body(): pl.pallas_call(functools.partial(body_kernel, trig), name='coulomb', out_...  30 us
    pallas_call x1, Pallas kernels, body(): pl.pallas_call(finish, name='finish', out_shape=jax.ShapeDtypeStruct((9,...  1.46 us

profile of v3, /device:TPU:33, one launch (start us, length us, event | category | flops | bytes accessed | tf_op | source)
XLA Modules:
  0.0 31.5 jit_solution(16733010661544205300)
XLA Ops:
  0.0 30.0 %coulomb.1.parts = f32[32,2,128]{2,1,0:T(2,128)} custom-call(f32[16,16,128]{2,1,0:T(8,128)} %bitcast.6, bf16[64,96]{1,0:T(8,128)(2,1)} %constant.10.clone.ly_in, bf16[32,192]{1,0:T(8,128)(2,1)} %constant.11.clone.lyi_in, bf16[2,256,512]{2,1,0:T(8,128)(2,1)} %constant.12.clone.bz_in, bf16[256,256]{1,0:T(8,128)(2,1)} %constant.13.clone.bzi_in, ...), custom_call_target="tpu_custom_call" | custom-call | tf_op jit(solution)/shard_map/coulomb/pallas_call | solution.py:416
  30.0 1.5 %finish.1 = f32[9,1,16]{2,1,0:T(1,128)} custom-call(f32[32,2,128]{2,1,0:T(2,128)} %coulomb.1.parts), custom_call_target="tpu_custom_call" | custom-call | tf_op jit(solution)/shard_map/finish/pallas_call | solution.py:452

commit v4 on v3

--- a/solution.py
+++ b/solution.py
@@ -15,7 +15,7 @@
 BF16 = jnp.bfloat16
 MESH = pl.DeviceIdType.MESH
 REACH = 4
-PIECES = 4
+PIECES = 2
 STEP = 16 // PIECES
 BEFORE = 12
 MIDDLE = 4
@@ -106,7 +106,7 @@
     trig,
     v_in, ly_in, lyi_in, bz_in, bzi_in, kt_in,
     rl,
-    u, pbuf, pl_in, vl, ly, lyi, bz, bzi, kt,
+    u, pbuf, pl_in, vl, vp, ly, lyi, bz, bzi, kt,
     m1, m2h, m2l, m3h, m3l, m4, m5, vh, vlo, sb,
     ready, ready_up, c_sem, a1_send, a1_recv, v_send, v_recv, v_loc, a2_send, a2_recv, a2_loc, r_send, r_recv, r_loc,
 ):
@@ -161,6 +161,22 @@
             greet(barrier, g + away, r)
             greet(barrier, sib + away, r)
 
+    @pl.when(plane == 1)
+    def _():
+        for away in (4, 12):
+            greet(barrier, g + away, r)
+            greet(barrier, sib + away, r)
+
+    @pl.when(plane == 2)
+    def _():
+        greet(barrier, g + 8, r)
+        greet(barrier, sib + 8, r)
+
+    @pl.when(plane == 7)
+    def _():
+        greet(barrier, g - 4, r)
+        greet(barrier, sib - 4, r)
+
     consts = [
         pltpu.make_async_copy(a, b, c_sem.at[i])
         for i, (a, b) in enumerate([(ly_in, ly), (lyi_in, lyi), (bz_in, bz), (bzi_in, bzi), (kt_in, kt)])
@@ -172,7 +188,7 @@
     )
     own.start()
 
-    across = jnp.where(plane > 0, 2, 0) + jnp.where(jnp.logical_or(plane == 4, plane == 7), 2, 0)
+    across = jnp.where(plane > 0, 2, 0) + jnp.where(plane > 2, 2, 0) + jnp.where(plane == 7, 2, 0)
     pl.semaphore_wait(barrier, 17 - n_later + across)
 
     for m, after in later:
@@ -182,6 +198,11 @@
     def _():
         greet(ready_up, up, r)
         greet(ready_up, up_sib, r)
+
+    @pl.when(plane == 3)
+    def _():
+        greet(ready_up, g - 4, r)
+        greet(ready_up, sib - 4, r)
 
     def block(d, part, k):
         return vl.at[pl.ds(pl.multiple_of(32 * d + 16 * part + STEP * k, STEP), STEP)]
@@ -203,22 +224,53 @@
         first.append(move(source(half, k), 1, 0, half, k, down))
         first.append(move(source(1 - half, k), 1, 1, half, k, down_sib))
     first += [move(source(1 - half, k), 0, 1, half, k, sib) for k in range(PIECES)]
-    passes = plane != 1
+    passes = jnp.logical_or(plane == 0, plane > 4)
     direct = []
     for k in range(PIECES):
         direct.append(move(source(half, k), REACH, 0, half, k, lax.rem(g + 8, 16), 1))
         direct.append(move(source(1 - half, k), REACH, 1, half, k, lax.rem(sib + 8, 16), 1))
 
+    def pass_block(part, k):
+        return vp.at[pl.ds(pl.multiple_of(16 * part + STEP * k, STEP), STEP)]
+
+    def pass_up(far, k):
+        vec = lax.rem((sib if far else g) + 4, 16)
+        return pltpu.make_async_remote_copy(
+            source(1 - half if far else half, k), pass_block(half, k),
+            v_send.at[sem_of(REACH + 1, far, k)], v_recv.at[sem_of(REACH + 1, far, k)],
+            device_id=(vec, r), device_id_type=MESH,
+        )
+
+    def pass_on(far, k):
+        part = 1 - half if far else half
+        return move(pass_block(part, k), REACH, far, part, k, lax.rem(g + 4, 16), 2)
+
+    pieces = [(far, k) for k in range(PIECES) for far in range(2)]
+    straight = jnp.logical_or(plane == 4, plane == 6)
+    upward = jnp.logical_or(plane == 5, plane == 7)
+    middle = jnp.logical_or(plane == 7, plane == 1)
+
+    def relay_up():
+        for far, k in pieces:
+            ref = pass_block(1 - half if far else half, k)
+            pltpu.make_async_copy(ref, ref, v_recv.at[sem_of(REACH + 1, far, k)]).wait()
+            pass_on(far, k).start()
+
     def start_down():
         for c in first[:2 * PIECES]:
             c.start()
 
     pl.when(plane > 0)(start_down)
 
-    @pl.when(plane == 4)
+    @pl.when(straight)
     def _():
         for c in direct:
             c.start()
+
+    @pl.when(upward)
+    def _():
+        for piece in pieces:
+            pass_up(*piece).start()
 
     pl.when(n_later > 0)(lambda: pl.semaphore_wait(ready, n_later))
 
@@ -236,6 +288,10 @@
     def _():
         pl.semaphore_wait(ready_up, 2)
         start_down()
+
+    @pl.when(plane == 1)
+    def _():
+        pl.semaphore_wait(ready_up, 2)
 
     def part_of(far):
         return 1 - half if far else half
@@ -259,6 +315,7 @@
                 pl.when(passes)(onward(*hop).start)
 
     relay(BEFORE)
+    pl.when(plane == 7)(relay_up)
     for c in consts:
         c.wait()
     pltpu.make_async_copy(u, u, a1_recv).wait()
@@ -347,6 +404,7 @@
             vh[32 * d:32 * d + 32, 128 * rho:128 * rho + 128] = hi
             vlo[32 * d:32 * d + 32, 128 * rho:128 * rho + 128] = lo
 
+    pl.when(plane == 1)(relay_up)
     relay(24 - BEFORE - MIDDLE)
     own.wait()
     for k in range(PIECES):
@@ -383,10 +441,20 @@
     for c in first:
         c.wait_send()
 
-    @pl.when(plane == 4)
+    @pl.when(straight)
     def _():
         for c in direct:
             c.wait_send()
+
+    @pl.when(upward)
+    def _():
+        for piece in pieces:
+            pass_up(*piece).wait_send()
+
+    @pl.when(middle)
+    def _():
+        for piece in pieces:
+            pass_on(*piece).wait_send()
 
     for d in range(1, REACH):
         for far in range(2):
@@ -424,6 +492,7 @@
             pltpu.VMEM((256, 128), F32),
             pltpu.VMEM((32, 8, 128), F32),
             pltpu.VMEM((160, 8, 128), F32),
+            pltpu.VMEM((32, 8, 128), F32),
             pltpu.VMEM(ly.shape, BF16),
             pltpu.VMEM(lyi.shape, BF16),
             pltpu.VMEM(bz.shape, BF16),
@@ -443,7 +512,7 @@
             pltpu.SemaphoreType.REGULAR,
             dma((5,)),
             dma, dma,
-            dma((12 * PIECES,)), dma((10 * PIECES,)), dma,
+            dma((14 * PIECES,)), dma((12 * PIECES,)), dma,
             dma, dma, dma,
             dma, dma, dma,
         ],

time: 31.6 us -> 31.1 us (0.984)
  Pallas kernels: 31.4 us -> 30.9 us
    pallas_call x1, Pallas kernels: 30 us -> 29.5 us  [body(): pl.pallas_call(functools.partial(body_kernel, trig), name='coulomb', out_...]
where the time goes in v4:
time: 31.1 us; the launch traced here: 30.9 us
  Pallas kernels  30.9 us (99%)
    pallas_call x1, Pallas kernels, body(): pl.pallas_call(functools.partial(body_kernel, trig), name='coulomb', out_...  29.5 us
    pallas_call x1, Pallas kernels, body(): pl.pallas_call(finish, name='finish', out_shape=jax.ShapeDtypeStruct((9,...  1.46 us

profile of v4, /device:TPU:33, one launch (start us, length us, event | category | flops | bytes accessed | tf_op | source)
XLA Modules:
  0.0 30.9 jit_solution(8096822705288025626)
XLA Ops:
  0.0 29.5 %coulomb.1.parts = f32[32,2,128]{2,1,0:T(2,128)} custom-call(f32[16,16,128]{2,1,0:T(8,128)} %bitcast.6, bf16[64,96]{1,0:T(8,128)(2,1)} %constant.10.clone.ly_in, bf16[32,192]{1,0:T(8,128)(2,1)} %constant.11.clone.lyi_in, bf16[2,256,512]{2,1,0:T(8,128)(2,1)} %constant.12.clone.bz_in, bf16[256,256]{1,0:T(8,128)(2,1)} %constant.13.clone.bzi_in, ...), custom_call_target="tpu_custom_call" | custom-call | tf_op jit(solution)/shard_map/coulomb/pallas_call | solution.py:484
  29.5 1.5 %finish.1 = f32[9,1,16]{2,1,0:T(1,128)} custom-call(f32[32,2,128]{2,1,0:T(2,128)} %coulomb.1.parts), custom_call_target="tpu_custom_call" | custom-call | tf_op jit(solution)/shard_map/finish/pallas_call | solution.py:521

commit v5 on v4

--- a/solution.py
+++ b/solution.py
@@ -138,9 +138,10 @@
 
     my_rank = rank(r // 4, lax.rem(r, 4) // 2, half)
     later = [
-        (m, (rank(m // 4, m % 4 // 2, 1 - half) > my_rank).astype(jnp.int32)) for m in range(16)
+        (m, (rank(m // 4, m % 4 // 2, 1 - half) > my_rank).astype(jnp.int32))
+        for m in range(0, 16, 2)
     ]
-    n_later = functools.reduce(lambda a, b: a + b, [after for _, after in later])
+    n_later = 2 * functools.reduce(lambda a, b: a + b, [after for _, after in later])
 
     def greet(sem, vec, to):
         pl.semaphore_signal(sem, inc=1, device_id=(vec, to), device_id_type=MESH)
@@ -153,7 +154,10 @@
         greet(barrier, up_sib, r)
 
     for m, after in later:
-        pl.when(after == 1)(functools.partial(greet, barrier, sib, m))
+        @pl.when(after == 1)
+        def _():
+            greet(barrier, sib, m)
+            greet(barrier, sib, m + 1)
 
     @pl.when(plane == 0)
     def _():
@@ -192,7 +196,10 @@
     pl.semaphore_wait(barrier, 17 - n_later + across)
 
     for m, after in later:
-        pl.when(after == 0)(functools.partial(greet, ready, sib, m))
+        @pl.when(after == 0)
+        def _():
+            greet(ready, sib, m)
+            greet(ready, sib, m + 1)
 
     @pl.when(plane == 7)
     def _():
@@ -281,8 +288,6 @@
             device_id=(sib, m), device_id_type=MESH,
         ).start()
 
-    for c in first[2 * PIECES:]:
-        c.start()
 
     @pl.when(plane == 0)
     def _():
@@ -319,6 +324,8 @@
     for c in consts:
         c.wait()
     pltpu.make_async_copy(u, u, a1_recv).wait()
+    for c in first[2 * PIECES:]:
+        c.start()
 
     lane = lax.broadcasted_iota(jnp.int32, (8, 128), 1) // 32
     odd1 = lane % 2 == 1
@@ -411,23 +418,27 @@
         wait_block(0, 1, k)
     for d in range(REACH):
         prepare(d)
-    for k in range(PIECES):
-        wait_block(REACH, 0, k)
-        wait_block(REACH, 1, k)
-    prepare(REACH)
-
     keep.wait()
     rest = pl_in.at[pl.ds(0, 31)]
     pltpu.make_async_copy(rest, rest, a2_recv).wait()
     parts = [split(pl_in[:, rho, :]) for rho in range(8)]
     ph = jnp.concatenate([p[0] for p in parts], axis=1)
     plo = jnp.concatenate([p[1] for p in parts], axis=1)
-    gram = dot_nt(ph, vh[...]) + dot_nt(plo, vh[...]) + dot_nt(ph, vlo[...])
+
+    def gram(rows):
+        return dot_nt(ph, vh[rows, :]) + dot_nt(plo, vh[rows, :]) + dot_nt(ph, vlo[rows, :])
+
+    near = gram(slice(0, 32 * REACH))
+    sb[0:16, 0, :] = near[0:16, :]
+    for k in range(PIECES):
+        wait_block(REACH, 0, k)
+        wait_block(REACH, 1, k)
+    prepare(REACH)
+    last = gram(slice(32 * REACH, 32 * REACH + 32))
     pad = jnp.zeros((16, 112), F32)
-    sb[0:16, 0, :] = gram[0:16, 0:128]
-    sb[0:16, 1, :] = jnp.concatenate([gram[0:16, 128:144], pad], axis=1)
-    sb[16:32, 0, :] = gram[16:32, 16:144]
-    sb[16:32, 1, :] = jnp.concatenate([gram[16:32, 144:160], pad], axis=1)
+    sb[0:16, 1, :] = jnp.concatenate([last[0:16, 0:16], pad], axis=1)
+    sb[16:32, 0, :] = jnp.concatenate([near[16:32, 16:128], last[16:32, 0:16]], axis=1)
+    sb[16:32, 1, :] = jnp.concatenate([last[16:32, 16:32], pad], axis=1)
 
     for vec, h, m in others():
         pltpu.make_async_remote_copy(

time: 31.1 us -> 31 us (level); the launches traced: 30.9 us -> 30.5 us
  Pallas kernels: 30.9 us -> 30.5 us
    pallas_call x1, Pallas kernels: 29.5 us -> 29 us  [body(): pl.pallas_call(functools.partial(body_kernel, trig), name='coulomb', out_...]
where the time goes in v5:
time: 31 us; the launch traced here: 30.5 us
  Pallas kernels  30.5 us (98%)
    pallas_call x1, Pallas kernels, body(): pl.pallas_call(functools.partial(body_kernel, trig), name='coulomb', out_...  29 us
    pallas_call x1, Pallas kernels, body(): pl.pallas_call(finish, name='finish', out_shape=jax.ShapeDtypeStruct((9,...  1.46 us

profile of v5, /device:TPU:33, one launch (start us, length us, event | category | flops | bytes accessed | tf_op | source)
XLA Modules:
  0.0 30.5 jit_solution(13215775579307589303)
XLA Ops:
  0.0 29.0 %coulomb.1.parts = f32[32,2,128]{2,1,0:T(2,128)} custom-call(f32[16,16,128]{2,1,0:T(8,128)} %bitcast.6, bf16[64,96]{1,0:T(8,128)(2,1)} %constant.10.clone.ly_in, bf16[32,192]{1,0:T(8,128)(2,1)} %constant.11.clone.lyi_in, bf16[2,256,512]{2,1,0:T(8,128)(2,1)} %constant.12.clone.bz_in, bf16[256,256]{1,0:T(8,128)(2,1)} %constant.13.clone.bzi_in, ...), custom_call_target="tpu_custom_call" | custom-call | tf_op jit(solution)/shard_map/coulomb/pallas_call | solution.py:495
  29.0 1.5 %finish.1 = f32[9,1,16]{2,1,0:T(1,128)} custom-call(f32[32,2,128]{2,1,0:T(2,128)} %coulomb.1.parts), custom_call_target="tpu_custom_call" | custom-call | tf_op jit(solution)/shard_map/finish/pallas_call | solution.py:532

commit v6 on v4

--- a/solution.py
+++ b/solution.py
@@ -374,25 +374,32 @@
         cols = slice(256 * n, 256 * n + 256)
         m5[:, cols] = dot(lyi[...], m4[:, cols])
 
-    sums = []
+    slot = (1 - half) * 16 + r
+    slots = []
     for part in range(2):
         vals = []
         for a in range(8):
             cols = slice((8 * part + a) * 128, (8 * part + a) * 128 + 128)
             vals += swap_chunks([m5[8 * j:8 * j + 8, cols] for j in range(4)], odd1, odd2)
-        sums.append(combine(trig[32 * part:32 * part + 32, 16:32].T, vals))
-    for n in range(16):
-        for x, val in ((16 + n, sums[0][n] + sums[1][n]), (15 - n, sums[0][n] - sums[1][n])):
-            pbuf[pl.ds(16 * (x // 2) + x % 2, 8, stride=2), :] = val
-
-    slot = (1 - half) * 16 + r
-
-    for vec, h, m in others():
+        slots.append(vals)
+
+    def send_potential(vec, h, m):
         rows = pl.multiple_of(16 * m + 8 * h, 8)
         pltpu.make_async_remote_copy(
             pbuf.at[pl.ds(rows, 8)], pl_in.at[slot], a2_send, a2_recv,
             device_id=(vec, m), device_id_type=MESH,
         ).start()
+
+    for n in range(16):
+        even, odd = [
+            combine(trig[32 * part:32 * part + 32, 16 + n:17 + n].T, slots[part])[0] for part in range(2)
+        ]
+        for x, val in ((16 + n, even + odd), (15 - n, even - odd)):
+            pbuf[pl.ds(16 * (x // 2) + x % 2, 8, stride=2), :] = val
+        if n % 2:
+            for m in (8 + n // 2, 7 - n // 2):
+                send_potential(sib, 1 - half, m)
+                pl.when(r != m)(functools.partial(send_potential, g, half, m))
     keep = pltpu.make_async_copy(
         pbuf.at[pl.ds(pl.multiple_of(16 * r + 8 * half, 8), 8)], pl_in.at[slot], a2_loc
     )

time: 31.1 us -> 31.1 us (level)
  no operation moved by 1% of the time
where the time goes in v6:
time: 31.1 us; the launch traced here: 30.9 us
  Pallas kernels  30.9 us (99%)
    pallas_call x1, Pallas kernels, body(): pl.pallas_call(functools.partial(body_kernel, trig), name='coulomb', out_...  29.5 us
    pallas_call x1, Pallas kernels, body(): pl.pallas_call(finish, name='finish', out_shape=jax.ShapeDtypeStruct((9,...  1.46 us

profile of v6, /device:TPU:33, one launch (start us, length us, event | category | flops | bytes accessed | tf_op | source)
XLA Modules:
  0.0 30.9 jit_solution(10973144931820768804)
XLA Ops:
  0.0 29.5 %coulomb.1.parts = f32[32,2,128]{2,1,0:T(2,128)} custom-call(f32[16,16,128]{2,1,0:T(8,128)} %bitcast.6, bf16[64,96]{1,0:T(8,128)(2,1)} %constant.10.clone.ly_in, bf16[32,192]{1,0:T(8,128)(2,1)} %constant.11.clone.lyi_in, bf16[2,256,512]{2,1,0:T(8,128)(2,1)} %constant.12.clone.bz_in, bf16[256,256]{1,0:T(8,128)(2,1)} %constant.13.clone.bzi_in, ...), custom_call_target="tpu_custom_call" | custom-call | tf_op jit(solution)/shard_map/coulomb/pallas_call | solution.py:491
  29.5 1.5 %finish.1 = f32[9,1,16]{2,1,0:T(1,128)} custom-call(f32[32,2,128]{2,1,0:T(2,128)} %coulomb.1.parts), custom_call_target="tpu_custom_call" | custom-call | tf_op jit(solution)/shard_map/finish/pallas_call | solution.py:528

commit v7 on v4

--- a/solution.py
+++ b/solution.py
@@ -17,8 +17,8 @@
 REACH = 4
 PIECES = 2
 STEP = 16 // PIECES
-BEFORE = 12
-MIDDLE = 4
+BEFORE = 10
+MIDDLE = 6
 
 
 def tables():

time: 31.1 us -> 31 us (level)
  no operation moved by 1% of the time
where the time goes in v7:
time: 31 us; the launch traced here: 30.9 us
  Pallas kernels  30.9 us (100%)
    pallas_call x1, Pallas kernels, body(): pl.pallas_call(functools.partial(body_kernel, trig), name='coulomb', out_...  29.4 us
    pallas_call x1, Pallas kernels, body(): pl.pallas_call(finish, name='finish', out_shape=jax.ShapeDtypeStruct((9,...  1.46 us

profile of v7, /device:TPU:33, one launch (start us, length us, event | category | flops | bytes accessed | tf_op | source)
XLA Modules:
  0.0 30.9 jit_solution(13580338345470902734)
XLA Ops:
  0.0 29.4 %coulomb.1.parts = f32[32,2,128]{2,1,0:T(2,128)} custom-call(f32[16,16,128]{2,1,0:T(8,128)} %bitcast.6, bf16[64,96]{1,0:T(8,128)(2,1)} %constant.10.clone.ly_in, bf16[32,192]{1,0:T(8,128)(2,1)} %constant.11.clone.lyi_in, bf16[2,256,512]{2,1,0:T(8,128)(2,1)} %constant.12.clone.bz_in, bf16[256,256]{1,0:T(8,128)(2,1)} %constant.13.clone.bzi_in, ...), custom_call_target="tpu_custom_call" | custom-call | tf_op jit(solution)/shard_map/coulomb/pallas_call | solution.py:484
  29.4 1.5 %finish.1 = f32[9,1,16]{2,1,0:T(1,128)} custom-call(f32[32,2,128]{2,1,0:T(2,128)} %coulomb.1.parts), custom_call_target="tpu_custom_call" | custom-call | tf_op jit(solution)/shard_map/finish/pallas_call | solution.py:521
